TPU v7x, 512 devices: a whole 4x8x8 slice. The times are simulated.
512 devices in a mesh: ctx: 32 (over z, x_hi, core), head: 16 (over y, x_lo).
Axes of the slice: x: 4 (x_hi: 2, x_lo: 2; x = x_hi * 2 + x_lo), y: 8, z: 8, core: 2. Of those that a mesh axis runs over, the one named last changes fastest.
Arguments:
- tokens: bfloat16 [131072, 1024], P(('ctx', 'head')), may hold values from -11 to 11
- ln_gain: float32 [1024], replicated, may hold values from 0.1 to 1.9
- ln_bias: float32 [1024], replicated, may hold values from -3 to 3
- qkv_weight: bfloat16 [1024, 16, 192], P(None, 'head'), may hold values from -7 to 7
- out_weight: bfloat16 [1024, 1024], P('head'), may hold values from -0.75 to 0.75
- output_bias_vector: float32 [1024], replicated, may hold values from -3 to 3
- lengths: int32 [1024], replicated, may hold values from 1 to 512, 131072 in all
- pairs_dev: int32 [1024, 3], replicated, may hold values from 0 to 31, all different within a row; in each aligned block of 32 rows (0 to 31, 32 to 63, ...) at most 4 rows name the same one
- pairs_off: int32 [1024, 3], replicated, may hold values from 0 to 31
Outputs:
- attended_out: bfloat16 [131072, 1024], P(('ctx', 'head'))
Inputs may be any that keep to these rules, and one draw needn't show every extreme that they name: The lengths sum to 131072. `pairs_dev`: each row names 3 different ctx indices; within the rows of one ctx index's 32 query blocks no ctx index is named more than 4 times.
All inputs are finite; a program needn't handle non-finite values.
Results may differ from a plain program's by a relative error of at most 0.0065.
The roundings to bfloat16 on the way count: a program that leaves them out, or rounds other values in their place, can miss the bound.
Values may be sent and summed in bfloat16 or wider, within the bound.
No kernel may reach another device: no remote copies, remote signals or barrier semaphores. Data moves between devices by JAX's collectives and lax.ppermute only.
A program may use at most 64 MiB of HBM per device.

v0:
```python
import math
import jax
import jax.numpy as jnp
from jax import lax
from jax.sharding import PartitionSpec as P

BLK = 128
RAND = 3
epsilon = 1e-05


def with_halo(cells, sides, width):
    for axis, dim in sides:
        count = lax.axis_size(axis)
        ends = count - 1
        head = lax.slice_in_dim(cells, 0, width, axis=dim)
        tail = lax.slice_in_dim(cells, cells.shape[dim] - width, cells.shape[dim], axis=dim)
        cells = jnp.concatenate(
            [
                lax.ppermute(tail, axis, [(i, (i + 1) % count) for i in range(ends)]),
                cells,
                lax.ppermute(head, axis, [((i + 1) % count, i) for i in range(ends)]),
            ],
            axis=dim,
        )
    return cells


def from_root(value, axis, source):
    kept = jnp.where(lax.axis_index(axis) == source, value, 0).astype(value.dtype)
    return lax.psum(kept, axis)


def normalize(tokens, ln_gain, ln_bias):
    values = tokens.astype(jnp.float32)
    center = values - jnp.mean(values, axis=-1, keepdims=True)
    spread = jnp.mean(center * center, axis=-1, keepdims=True)
    return (center * lax.rsqrt(spread + epsilon) * ln_gain + ln_bias).astype(jnp.bfloat16)


def owning_line(line_end, positions):
    span_rows = positions.shape[0]
    step_rows = math.gcd(span_rows, 512)
    blocked = positions.reshape(span_rows // step_rows, step_rows)

    def count_ends(block_pos):
        return jnp.sum((line_end[None, :] <= block_pos[:, None]).astype(jnp.int32), axis=1)

    return lax.map(count_ends, blocked).reshape(span_rows)


def attend(queries, window_rows, window_line, query_line, global_kv, random_kv, head_dim):
    group_size = queries.shape[0]
    block_rows = queries.shape[1]
    windows = jnp.stack(
        [
            window_rows[member * block_rows : (member + 3) * block_rows]
            for member in range(group_size)
        ]
    )
    window_ids = jnp.stack(
        [
            window_line[member * block_rows : (member + 3) * block_rows]
            for member in range(group_size)
        ]
    )
    global_rows = jnp.broadcast_to(global_kv[None], (group_size,) + global_kv.shape)
    key_rows = jnp.concatenate([windows, global_rows, random_kv], axis=1)
    key_part = key_rows[..., :head_dim]
    value_part = key_rows[..., head_dim:]
    scores = jnp.einsum(
        "gqhd,gkhd->ghqk", queries, key_part, preferred_element_type=jnp.float32
    ) * head_dim ** (-0.5)
    allowed_window = window_ids[:, None, :] == query_line[:, :, None]
    extra_keys = key_rows.shape[1] - 3 * block_rows
    allowed = jnp.concatenate(
        [allowed_window, jnp.ones((group_size, block_rows, extra_keys), dtype=bool)], axis=2
    )
    scores = jnp.where(allowed[:, None], scores, -jnp.inf)
    row_max = jnp.max(scores, axis=-1, keepdims=True)
    exp_scores = jnp.exp(scores - row_max)
    denominator = jnp.sum(exp_scores, axis=-1)
    rounded = exp_scores.astype(jnp.bfloat16)
    summed = jnp.einsum("ghqk,gkhd->gqhd", rounded, value_part, preferred_element_type=jnp.float32)
    return (summed / jnp.transpose(denominator, (0, 2, 1))[..., None]).astype(jnp.bfloat16)


def per_device(
    tokens,
    ln_gain,
    ln_bias,
    qkv_weight,
    out_weight,
    output_bias_vector,
    lengths,
    pairs_dev,
    pairs_off,
):
    ctx_count = lax.axis_size("ctx")
    ctx_index = lax.axis_index("ctx")
    normed = normalize(tokens, ln_gain, ln_bias)
    local_heads = qkv_weight.shape[1]
    head_dim = qkv_weight.shape[2] // 3
    every_head = jnp.einsum(
        "td,dhc->thc",
        normed,
        lax.all_gather(qkv_weight, "head", axis=1, tiled=True),
        preferred_element_type=jnp.float32,
    ).astype(jnp.bfloat16)
    projected_qkv = lax.all_to_all(every_head, "head", split_axis=1, concat_axis=0, tiled=True)
    ctx_rows = projected_qkv.shape[0]
    blocks_dev = ctx_rows // BLK
    q_blocks = projected_qkv[..., :head_dim].reshape(blocks_dev, BLK, local_heads, head_dim)
    kv_width = local_heads * 2 * head_dim
    flat_kv = projected_qkv[..., head_dim:].reshape(ctx_rows, kv_width)
    padded = with_halo(flat_kv, (("ctx", 0),), BLK)
    padded = padded.reshape(ctx_rows + 2 * BLK, local_heads, 2 * head_dim)
    global_kv = from_root(flat_kv[:BLK], "ctx", 0).reshape(BLK, local_heads, 2 * head_dim)
    pair_count = blocks_dev * RAND
    capacity = max(2, (pair_count * 4 + 3 * ctx_count - 1) // (3 * ctx_count))
    all_dev = pairs_dev.reshape(ctx_count, pair_count)
    all_off = pairs_off.reshape(ctx_count, pair_count)
    own_pairs = all_dev == ctx_index
    pair_order = jnp.arange(pair_count, dtype=jnp.int32)
    lower_tri = pair_order[None, :] < pair_order[:, None]
    slot_rank = jnp.sum((own_pairs[:, None, :] & lower_tri[None]).astype(jnp.int32), axis=2)
    slot_ids = jnp.arange(capacity, dtype=jnp.int32)
    selected_items = own_pairs[:, None, :] & (slot_rank[:, None, :] == slot_ids[None, :, None])
    block_ids = jnp.arange(blocks_dev, dtype=jnp.int32)
    shifted_popular = (all_off[:, :, None] == block_ids[None, None, :]).astype(jnp.bfloat16)
    send_hot = jnp.einsum(
        "utk,ukv->utv",
        selected_items.astype(jnp.bfloat16),
        shifted_popular,
        preferred_element_type=jnp.float32,
    )
    send_hot = send_hot.astype(jnp.bfloat16).reshape(ctx_count * capacity, blocks_dev)
    kv_blocks = flat_kv.reshape(blocks_dev, BLK * kv_width)
    outgoing = jnp.dot(send_hot, kv_blocks, preferred_element_type=jnp.float32).astype(jnp.bfloat16)
    outgoing = outgoing.reshape(ctx_count, capacity, BLK, kv_width)
    incoming = lax.all_to_all(outgoing, "ctx", split_axis=0, concat_axis=0, tiled=True).reshape(
        ctx_count * capacity, BLK * kv_width
    )
    own_dev = all_dev[ctx_index]
    earlier = (own_dev[:, None] == own_dev[None, :]) & lower_tri
    position = own_dev * capacity + jnp.sum(earlier.astype(jnp.int32), axis=1)
    slot_every_block = jnp.arange(ctx_count * capacity, dtype=jnp.int32)
    take_hot = (position[:, None] == slot_every_block[None, :]).astype(jnp.bfloat16)
    random_every_block = jnp.dot(take_hot, incoming, preferred_element_type=jnp.float32).astype(
        jnp.bfloat16
    )
    random_every_block = random_every_block.reshape(
        blocks_dev, RAND * BLK, local_heads, 2 * head_dim
    )
    line_end = jnp.cumsum(lengths)
    doc_tokens = ctx_count * ctx_rows
    positions = ctx_index * ctx_rows - BLK + jnp.arange(ctx_rows + 2 * BLK, dtype=jnp.int32)
    inside = (positions >= 0) & (positions < doc_tokens)
    ext_line = jnp.where(inside, owning_line(line_end, jnp.clip(positions, 0, doc_tokens - 1)), -1)
    group_size = math.gcd(blocks_dev, 4)

    def group_step(group_index):
        first_block = group_index * group_size
        window_rows = lax.dynamic_slice_in_dim(padded, first_block * BLK, (group_size + 2) * BLK, 0)
        window_line = lax.dynamic_slice_in_dim(
            ext_line, first_block * BLK, (group_size + 2) * BLK, 0
        )
        query_line = lax.dynamic_slice_in_dim(
            ext_line, (first_block + 1) * BLK, group_size * BLK, 0
        ).reshape(group_size, BLK)
        queries = lax.dynamic_slice_in_dim(q_blocks, first_block, group_size, 0)
        random_kv = lax.dynamic_slice_in_dim(random_every_block, first_block, group_size, 0)
        return attend(queries, window_rows, window_line, query_line, global_kv, random_kv, head_dim)

    attended = lax.map(group_step, jnp.arange(blocks_dev // group_size, dtype=jnp.int32))
    attended = attended.reshape(ctx_rows, local_heads * head_dim)
    rows_back = lax.all_to_all(attended, "head", split_axis=0, concat_axis=1, tiled=True)
    projected = jnp.dot(
        rows_back,
        lax.all_gather(out_weight, "head", axis=0, tiled=True),
        preferred_element_type=jnp.float32,
    )
    return (projected + output_bias_vector).astype(jnp.bfloat16)


def solution(mesh):
    in_specs = (
        P(("ctx", "head"), None),
        P(),
        P(),
        P(None, "head", None),
        P("head", None),
        P(),
        P(),
        P(),
        P(),
    )
    out_specs = P(("ctx", "head"), None)
    return jax.shard_map(
        per_device, mesh=mesh, in_specs=in_specs, out_specs=out_specs, check_vma=False
    )
```

profile of v0, /device:TPU:197, one launch (start us, length us, event | category | flops | bytes accessed | tf_op | source)
XLA Modules:
  0.0 548.6 jit_solution(13660856780126761549)
XLA Ops:
  6.5 0.7 all-gather.3.cloned.1.call-update
  7.3 1.2 convert_reduce_fusion.2
  8.5 1.3 fusion.13
  9.8 144.3 %all-gather.3.cloned.1.call-done = bf16[1024,16,192]{0,2,1:T(8,128)(2,1)} async-done(((bf16[1024,1,192]{0,2,1:T(8,128)(2,1)}), bf16[1024,16,192]{0,2,1:T(8,128)(2,1)}) %all-gather.3.cloned.1.call-update) | async-done | bytes 6291472 | tf_op jit(solution)/shard_map/all_gather | solution.py:107
  154.1 5.0 fusion.17
  159.1 1.4 convert_element_type.53
  160.5 7.6 %all-to-all-start = ((bf16[256,16,192]{0,2,1:T(8,128)(2,1)}), bf16[256,16,192]{0,2,1:T(8,128)(2,1)S(1)}, u32[]{:S(2)}, u32[]{:S(2)}) async-start(bf16[256,16,192]{0,2,1:T(8,128)(2,1)} %convert_element_type.53), calls=%async_computation | async-start | bytes 3145728 | tf_op jit(solution)/shard_map/all_to_all | solution.py:110
  169.1 0.6 convert_reduce_fusion.1
  170.0 34.0 %all-to-all-done = bf16[256,16,192]{0,2,1:T(8,128)(2,1)S(1)} async-done(((bf16[256,16,192]{0,2,1:T(8,128)(2,1)}), bf16[256,16,192]{0,2,1:T(8,128)(2,1)S(1)}, u32[]{:S(2)}, u32[]{:S(2)}) %all-to-all-start) | async-done | bytes 1572896 | tf_op jit(solution)/shard_map/all_to_all | solution.py:110
  204.2 1.3 fusion.35
  205.5 2.3 copy.42
  207.8 2.3 reshape_reshape.3
  210.1 2.4 fusion.9
  212.5 3.2 copy.52
  215.7 14.4 %all-to-all-start.1 = ((bf16[32,4,128,128]{3,2,1,0:T(8,128)(2,1)}), bf16[32,4,128,128]{3,2,1,0:T(8,128)(2,1)}, u32[]{:S(2)}, u32[]{:S(2)}) async-start(bf16[32,4,128,128]{3,2,1,0:T(8,128)(2,1)} %bitcast.131), calls=%async_computation.1 | async-start | bytes 8388608 | tf_op jit(solution)/shard_map/all_to_all | solution.py:141
  230.2 0.7 all-gather.5.cloned.1.call-update
  231.5 5.6 %while.24 = (s32[]{:T(128)}, s32[17,256]{1,0:T(8,128)S(1)}, s32[1024]{0:T(1024)S(1)}, s32[17,256]{1,0:T(8,128)S(1)}) while((s32[]{:T(128)}, s32[17,256]{1,0:T(8,128)S(1)}, s32[1024]{0:T(1024)S(1)}, s32[17,256]{1,0:T(8,128)S(1)}) %tuple.67), condition=%wide.region_6.7_spmd.clone, body=%wide.region_4.0_spmd.sunk.clone | while | flops 786178 | bytes 10301 | solution.py:49
  237.3 4.6 collective-permute-start
  241.9 1.9 collective-permute-start.1
  243.9 0.9 copy.54
  244.8 199.1 %psum.7 = bf16[128,128]{0,1:T(8,128)(2,1)S(1)} all-reduce(bf16[128,128]{0,1:T(8,128)(2,1)S(1)} %broadcast_select_fusion), channel_id=1, replica_groups=mesh['ctx'=32,'head'=16] {'ctx'}, use_global_device_ids=true, to_apply=%region_9.10 | all-reduce | flops 16384 | bytes 65536 | tf_op jit(solution)/shard_map/psum | solution.py:31
  443.9 1.1 maximum_bitcast_fusion
  445.0 5.1 convolution_convert_fusion.1
  450.1 3.4 reshape.152
  453.5 62.3 %while.25 = (s32[]{:T(128)}, bf16[8,4,128,1,64]{2,1,0,4,3:T(4,128)(2,1)}, s32[8]{0:T(128)S(1)}, bf16[4352,1,128]{0,2,1:T(8,128)(2,1)}, bf16[128,128]{0,1:T(8,128...) while((s32[]{:T(128)}, ...), condition=%wide.region_13.14_spmd.clone, body=%wide.region_10.13_spmd.sunk.clone | while | flops 126422544 | bytes 11633483 | solution.py:175
  454.6 1.1 dynamic-slice_bitcast_fusion.10
  456.3 1.0 constant_dynamic-slice_fusion.10
  458.1 0.9 constant_dynamic-slice_fusion.11
  460.6 0.7 copy_dynamic-update-slice_fusion.3
  462.4 1.1 dynamic-slice_bitcast_fusion.10
  464.1 1.0 constant_dynamic-slice_fusion.10
  465.9 0.9 constant_dynamic-slice_fusion.11
  467.8 0.6 fusion.55
  468.4 0.7 copy_dynamic-update-slice_fusion.3
  470.2 1.1 dynamic-slice_bitcast_fusion.10
  471.9 1.0 constant_dynamic-slice_fusion.10
  473.6 0.9 constant_dynamic-slice_fusion.11
  476.2 0.7 copy_dynamic-update-slice_fusion.3
  478.0 1.1 dynamic-slice_bitcast_fusion.10
  479.6 1.0 constant_dynamic-slice_fusion.10
  481.4 0.9 constant_dynamic-slice_fusion.11
  483.4 0.6 fusion.55
  484.0 0.7 copy_dynamic-update-slice_fusion.3
  485.8 1.1 dynamic-slice_bitcast_fusion.10
  487.4 1.0 constant_dynamic-slice_fusion.10
  489.2 0.9 constant_dynamic-slice_fusion.11
  491.8 0.7 copy_dynamic-update-slice_fusion.3
  493.5 1.1 dynamic-slice_bitcast_fusion.10
  495.2 1.0 constant_dynamic-slice_fusion.10
  497.0 0.9 constant_dynamic-slice_fusion.11
  499.5 0.7 copy_dynamic-update-slice_fusion.3
  501.3 1.1 dynamic-slice_bitcast_fusion.10
  503.0 1.0 constant_dynamic-slice_fusion.10
  504.8 0.9 constant_dynamic-slice_fusion.11
  507.3 0.7 copy_dynamic-update-slice_fusion.3
  509.1 1.1 dynamic-slice_bitcast_fusion.10
  510.8 1.0 constant_dynamic-slice_fusion.10
  512.6 0.9 constant_dynamic-slice_fusion.11
  515.1 0.7 copy_dynamic-update-slice_fusion.3
  515.8 1.4 all_to_all.35
  517.2 1.0 copy.46
  518.1 3.6 all-to-all-start.2
  521.7 16.8 %all-to-all-done.2 = bf16[16,256,64]{1,2,0:T(8,128)(2,1)S(1)} async-done(((bf16[16,256,64]{1,2,0:T(8,128)(2,1)}), bf16[16,256,64]{1,2,0:T(8,128)(2,1)S(1)}, u32[]{:S(2)}, u32[]{:S(2)}) %all-to-all-start.2) | async-done | bytes 524320 | tf_op jit(solution)/shard_map/all_to_all | solution.py:177
  538.6 3.1 fusion.10
  (218 shorter events, 28.9 us)
Async XLA Ops:
  6.5 147.5 %all-gather.3.cloned.1.call-start = ((), (), s32[]{:S(2)}) async-start(), calls=%async_computation.3 | async-start | bytes 6684672 | tf_op jit(solution)/shard_map/all_gather | solution.py:107
  160.5 7.6 %copy-start.1 = (s32[1024,3]{0,1:T(4,128)S(1)}, s32[1024,3]{0,1:T(4,128)}, u32[]{:S(2)}) copy-start(s32[1024,3]{0,1:T(4,128)} %param.20) | copy-start | bytes 36868
  160.5 8.1 %copy-start.2 = (s32[1024,3]{0,1:T(4,128)S(1)}, s32[1024,3]{0,1:T(4,128)}, u32[]{:S(2)}) copy-start(s32[1024,3]{0,1:T(4,128)} %param.21) | copy-start | bytes 36868
  160.5 43.5 %all-to-all-start = ((bf16[256,16,192]{0,2,1:T(8,128)(2,1)}), bf16[256,16,192]{0,2,1:T(8,128)(2,1)S(1)}, u32[]{:S(2)}, u32[]{:S(2)}) async-start(bf16[256,16,192]{0,2,1:T(8,128)(2,1)} %convert_element_type.53), calls=%async_computation | async-start | bytes 3145728 | tf_op jit(solution)/shard_map/all_to_all | solution.py:110
  215.7 15.2 %copy-start.3 = (s32[1024]{0:T(1024)S(1)}, s32[1024]{0:T(1024)}, u32[]{:S(2)}) copy-start(s32[1024]{0:T(1024)} %param.19) | copy-start | bytes 12292
  215.7 229.2 %all-to-all-start.1 = ((bf16[32,4,128,128]{3,2,1,0:T(8,128)(2,1)}), bf16[32,4,128,128]{3,2,1,0:T(8,128)(2,1)}, u32[]{:S(2)}, u32[]{:S(2)}) async-start(bf16[32,4,128,128]{3,2,1,0:T(8,128)(2,1)} %bitcast.131), calls=%async_computation.1 | async-start | bytes 8388608 | tf_op jit(solution)/shard_map/all_to_all | solution.py:141
  230.1 291.6 %all-gather.5.cloned.1.call-start = ((), (), s32[]{:S(2)}) async-start(), calls=%async_computation.4 | async-start | bytes 2228224 | tf_op jit(solution)/shard_map/all_gather | solution.py:180
  237.3 206.6 %collective-permute-start = (bf16[128,128]{0,1:T(8,128)(2,1)S(1)}, bf16[128,128]{0,1:T(8,128)(2,1)S(1)}, u32[]{:S(2)}, u32[]{:S(2)}) collective-permute-start(bf16[128,128]{0,1:T(8,128)(2,1)S(1)} %get-tuple-element.198), channel_id=1, source_target_pairs={{0,16},{16,32},{32,48},{48,64},{64,80},{80,96},{96,112},{112,128},... | collective-permute-start | bytes 98312 | tf_op jit(solution)/shard_map/ppermute | solution.py:20
  241.9 202.0 %collective-permute-start.1 = (bf16[128,128]{0,1:T(8,128)(2,1)S(1)}, bf16[128,128]{0,1:T(8,128)(2,1)S(1)}, u32[]{:S(2)}, u32[]{:S(2)}) collective-permute-start(bf16[128,128]{0,1:T(8,128)(2,1)S(1)} %get-tuple-element.199), channel_id=1, source_target_pairs={{16,0},{32,16},{48,32},{64,48},{80,64},{96,80},{112,96},{128,112},... | collective-permute-start | bytes 98312 | tf_op jit(solution)/shard_map/ppermute | solution.py:22
  515.8 22.8 %copy-start = (f32[1024]{0:T(1024)S(1)}, f32[1024]{0:T(1024)}, u32[]{:S(2)}) copy-start(f32[1024]{0:T(1024)} %param.18) | copy-start | bytes 12292
  518.1 20.5 %all-to-all-start.2 = ((bf16[16,256,64]{1,2,0:T(8,128)(2,1)}), bf16[16,256,64]{1,2,0:T(8,128)(2,1)S(1)}, u32[]{:S(2)}, u32[]{:S(2)}) async-start(bf16[16,256,64]{1,2,0:T(8,128)(2,1)} %copy.46), calls=%async_computation.2 | async-start | bytes 1048576 | tf_op jit(solution)/shard_map/all_to_all | solution.py:177
Sparse Core Ops, SparseCore 0:
  9.4 144.5 all-gather.2
  233.0 95.7 all-gather.4
where the time goes:
time: 550 us; the launch traced here: 549 us
  blocking collectives  199 us (36%)
  waiting for transfers between devices  197 us (36%)
  local copies, waits for them, and re-layouts  55.9 us (10%)
  starting transfers between devices  32.1 us (6%)
  matrix products  24.9 us (5%)
  other arithmetic  16.3 us (3%)
  between operations  13.7 us (2%)
  loops' own time  10 us (2%)
    psum x1, blocking collectives, from_root(): return lax.psum(kept, axis)  199 us
    all_gather x1, waiting for transfers between devices, per_device(): lax.all_gather(qkv_weight, 'head', axis=1, tiled=True)  144 us
    all_to_all x1, waiting for transfers between devices, per_device(): lax.all_to_all(every_head, 'head', split_axis=1, concat_axis=0, tiled=True)  34 us
    all_to_all x1, waiting for transfers between devices, per_device(): lax.all_to_all(attended, 'head', split_axis=0, concat_axis=1, tiled=True)  16.8 us
    all_to_all x1, starting transfers between devices, per_device(): lax.all_to_all(outgoing, 'ctx', split_axis=0, concat_axis=0, tiled=True)  14.4 us
  transfers between devices with their start and end apart: 7, of which 3 were waited for; matrix products, arithmetic and copies ran while one was open for 14% of the time, Pallas kernels for 0%

commit v1 on v0

--- a/solution.py
+++ b/solution.py
@@ -28,7 +28,7 @@
 
 def from_root(value, axis, source):
     kept = jnp.where(lax.axis_index(axis) == source, value, 0).astype(value.dtype)
-    return lax.psum(kept, axis)
+    return jnp.sum(lax.all_gather(kept, axis), axis=0)
 
 
 def normalize(tokens, ln_gain, ln_bias):

time: 550 us -> 442 us (0.80)
  the two profiles are of different devices: /device:TPU:197 before, /device:TPU:4 now
where the time goes in v1:
time: 442 us; the launch traced here: 441 us
  waiting for transfers between devices  285 us (64%)
  local copies, waits for them, and re-layouts  58.2 us (13%)
  starting transfers between devices  29.1 us (7%)
  matrix products  24.9 us (6%)
  other arithmetic  17.4 us (4%)
  between operations  13.4 us (3%)
  loops' own time  12.3 us (3%)
    all_gather x1, waiting for transfers between devices, per_device(): lax.all_gather(qkv_weight, 'head', axis=1, tiled=True)  147 us
    all_gather x1, waiting for transfers between devices, from_root(): return jnp.sum(lax.all_gather(kept, axis), axis=0)  61.7 us
    all_to_all x1, waiting for transfers between devices, per_device(): lax.all_to_all(every_head, 'head', split_axis=1, concat_axis=0, tiled=True)  37.3 us
    all_to_all x1, waiting for transfers between devices, per_device(): lax.all_to_all(outgoing, 'ctx', split_axis=0, concat_axis=0, tiled=True)  18.1 us
    all_to_all x1, waiting for transfers between devices, per_device(): lax.all_to_all(attended, 'head', split_axis=0, concat_axis=1, tiled=True)  17.8 us
    another operation x1, loops' own time, per_device(): lax.map(group_step, jnp.arange(blocks_dev // group_size, dtype=jnp.int32))  11.8 us
    all_to_all x1, starting transfers between devices, per_device(): lax.all_to_all(outgoing, 'ctx', split_axis=0, concat_axis=0, tiled=True)  10.7 us
    dynamic_slice x16, local copies, waits for them, and re-layouts, group_step(): lax.dynamic_slice_in_dim(random_every_block, first_block, group_size, 0)  9.99 us
  transfers between devices with their start and end apart: 8, of which 6 were waited for; matrix products, arithmetic and copies ran while one was open for 19% of the time, Pallas kernels for 0%

profile of v1, /device:TPU:4, one launch (start us, length us, event | category | flops | bytes accessed | tf_op | source)
XLA Modules:
  0.0 440.5 jit_solution(14997889441972672063)
XLA Ops:
  6.5 0.7 all-gather.5.cloned.1.call-update
  7.3 1.2 convert_reduce_fusion.2
  8.5 1.3 fusion.13
  9.8 147.1 %all-gather.5.cloned.1.call-done = bf16[1024,16,192]{0,2,1:T(8,128)(2,1)} async-done(((bf16[1024,1,192]{0,2,1:T(8,128)(2,1)}), bf16[1024,16,192]{0,2,1:T(8,128)(2,1)}) %all-gather.5.cloned.1.call-update) | async-done | bytes 6291472 | tf_op jit(solution)/shard_map/all_gather | solution.py:107
  156.9 5.0 %fusion.17 = f32[256,3072]{0,1:S(1)} fusion(bf16[1024,3072]{0,1:T(8,128)(2,1)} %bitcast.148, bf16[256,1024]{1,0:T(8,128)(2,1)} %param.13, f32[1024]{0:T(1024)} %param.15, f32[1024]{0:T(1024)} %param.14, f32[256]{0:T(256)S(1)} %add_rsqrt_fusion, f32[256]{0:T(256)S(1)} %broadcast_multiply_fusion), kind=kOutput, calls=%fused_computation.44 | convolution fusion | flops 1612185600 | bytes 9971712
  162.0 1.4 convert_element_type.55
  163.3 7.5 %all-to-all-start = ((bf16[256,16,192]{0,2,1:T(8,128)(2,1)}), bf16[256,16,192]{0,2,1:T(8,128)(2,1)S(1)}, u32[]{:S(2)}, u32[]{:S(2)}) async-start(bf16[256,16,192]{0,2,1:T(8,128)(2,1)} %convert_element_type.55), calls=%async_computation | async-start | bytes 3145728 | tf_op jit(solution)/shard_map/all_to_all | solution.py:110
  172.9 37.3 %all-to-all-done = bf16[256,16,192]{0,2,1:T(8,128)(2,1)S(1)} async-done(((bf16[256,16,192]{0,2,1:T(8,128)(2,1)}), bf16[256,16,192]{0,2,1:T(8,128)(2,1)S(1)}, u32[]{:S(2)}, u32[]{:S(2)}) %all-to-all-start) | async-done | bytes 1572896 | tf_op jit(solution)/shard_map/all_to_all | solution.py:110
  210.3 1.2 fusion.35
  211.5 2.3 copy.42
  213.8 2.3 reshape_reshape.3
  216.8 2.5 fusion.9
  219.2 3.2 copy.54
  222.4 10.7 %all-to-all-start.1 = ((bf16[32,4,128,128]{3,2,1,0:T(8,128)(2,1)}), bf16[32,4,128,128]{3,2,1,0:T(8,128)(2,1)}, u32[]{:S(2)}, u32[]{:S(2)}) async-start(bf16[32,4,128,128]{3,2,1,0:T(8,128)(2,1)} %bitcast.135), calls=%async_computation.1 | async-start | bytes 8388608 | tf_op jit(solution)/shard_map/all_to_all | solution.py:141
  233.2 0.7 all-gather.7.cloned.1.call-update
  234.5 5.6 %while.24 = (s32[]{:T(128)}, s32[17,256]{1,0:T(8,128)S(1)}, s32[1024]{0:T(1024)S(1)}, s32[17,256]{1,0:T(8,128)S(1)}) while((s32[]{:T(128)}, s32[17,256]{1,0:T(8,128)S(1)}, s32[1024]{0:T(1024)S(1)}, s32[17,256]{1,0:T(8,128)S(1)}) %tuple.68), condition=%wide.region_6.7_spmd.clone, body=%wide.region_4.0_spmd.sunk.clone | while | flops 786178 | bytes 10301 | solution.py:49
  240.3 2.0 collective-permute-start
  242.3 5.2 %collective-permute-start.1 = (bf16[128,128]{0,1:T(8,128)(2,1)S(1)}, bf16[128,128]{0,1:T(8,128)(2,1)S(1)}, u32[]{:S(2)}, u32[]{:S(2)}) collective-permute-start(bf16[128,128]{0,1:T(8,128)(2,1)S(1)} %get-tuple-element.199), channel_id=1, source_target_pairs={{16,0},{32,16},{48,32},{64,48},{80,64},{96,80},{112,96},{128,112},... | collective-permute-start | bytes 98312 | tf_op jit(solution)/shard_map/ppermute | solution.py:22
  247.6 0.9 copy.56
  248.5 1.7 collective-permute-done.1
  250.3 1.1 maximum_bitcast_fusion
  251.3 61.7 %all-gather.9.cloned.1.call-done = bf16[4096,1,128]{0,2,1:T(8,128)(2,1)} async-done(((bf16[128,1,128]{0,2,1:T(8,128)(2,1)}), bf16[4096,1,128]{0,2,1:T(8,128)(2,1)}) %all-gather.9.cloned.1.call-update) | async-done | bytes 1048592 | tf_op jit(solution)/shard_map/all_gather | solution.py:31
  313.1 1.4 copy.53
  315.0 18.1 %all-to-all-done.1 = bf16[32,4,128,128]{3,2,1,0:T(8,128)(2,1)} async-done(((bf16[32,4,128,128]{3,2,1,0:T(8,128)(2,1)}), bf16[32,4,128,128]{3,2,1,0:T(8,128)(2,1)}, u32[]{:S(2)}, u32[]{:S(2)}) %all-to-all-start.1) | async-done | bytes 4194336 | tf_op jit(solution)/shard_map/all_to_all | solution.py:141
  333.1 5.1 %convolution_convert_fusion.1 = bf16[96,16384]{1,0:T(8,128)(2,1)S(1)} fusion(bf16[16,8,128,128]{3,2,1,0:T(8,128)(2,1)} %bitcast.50, s32[96]{0:T(128)S(1)} %multiply_add_fusion), kind=kOutput, calls=%fused_computation.26 | convolution fusion | flops 404238336 | bytes 7340416 | tf_op jit(solution)/shard_map/dot_general | solution.py:149
  338.2 3.4 reshape.165
  341.6 65.5 %while.25 = (s32[]{:T(128)}, bf16[8,4,128,1,64]{2,1,0,4,3:T(4,128)(2,1)}, s32[8]{0:T(128)S(1)}, bf16[4352,1,128]{0,2,1:T(8,128)(2,1)}, bf16[128,128]{0,1:T(8,128...) while((s32[]{:T(128)}, ...), condition=%wide.region_13.14_spmd.clone, body=%wide.region_10.13_spmd.sunk.clone | while | flops 126422544 | bytes 11633483 | solution.py:175
  343.0 1.1 dynamic-slice_bitcast_fusion.10
  344.8 1.0 constant_dynamic-slice_fusion.10
  346.6 0.9 constant_dynamic-slice_fusion.11
  349.2 0.7 copy_dynamic-update-slice_fusion.3
  351.2 1.1 dynamic-slice_bitcast_fusion.10
  353.0 1.0 constant_dynamic-slice_fusion.10
  354.8 0.9 constant_dynamic-slice_fusion.11
  357.3 0.7 copy_dynamic-update-slice_fusion.3
  359.4 1.1 dynamic-slice_bitcast_fusion.10
  361.2 1.0 constant_dynamic-slice_fusion.10
  363.0 0.9 constant_dynamic-slice_fusion.11
  365.5 0.7 copy_dynamic-update-slice_fusion.3
  367.6 1.1 dynamic-slice_bitcast_fusion.10
  369.4 1.0 constant_dynamic-slice_fusion.10
  371.2 0.9 constant_dynamic-slice_fusion.11
  373.7 0.7 copy_dynamic-update-slice_fusion.3
  375.8 1.1 dynamic-slice_bitcast_fusion.10
  377.6 1.0 constant_dynamic-slice_fusion.10
  379.4 1.0 constant_dynamic-slice_fusion.11
  381.9 0.7 copy_dynamic-update-slice_fusion.3
  384.0 1.1 dynamic-slice_bitcast_fusion.10
  385.8 1.0 constant_dynamic-slice_fusion.10
  387.5 0.9 constant_dynamic-slice_fusion.11
  390.1 0.7 copy_dynamic-update-slice_fusion.3
  392.1 1.1 dynamic-slice_bitcast_fusion.10
  393.9 1.0 constant_dynamic-slice_fusion.10
  395.7 0.9 constant_dynamic-slice_fusion.11
  398.3 0.7 copy_dynamic-update-slice_fusion.3
  400.3 1.1 dynamic-slice_bitcast_fusion.10
  402.1 1.0 constant_dynamic-slice_fusion.10
  403.9 0.9 constant_dynamic-slice_fusion.11
  406.4 0.7 copy_dynamic-update-slice_fusion.3
  407.1 1.4 all_to_all.35
  408.5 1.0 copy.46
  409.5 3.6 all-to-all-start.2
  413.1 17.8 %all-to-all-done.2 = bf16[16,256,64]{1,2,0:T(8,128)(2,1)S(1)} async-done(((bf16[16,256,64]{1,2,0:T(8,128)(2,1)}), bf16[16,256,64]{1,2,0:T(8,128)(2,1)S(1)}, u32[]{:S(2)}, u32[]{:S(2)}) %all-to-all-start.2) | async-done | bytes 524320 | tf_op jit(solution)/shard_map/all_to_all | solution.py:177
  430.9 3.1 fusion.10
  (221 shorter events, 32.7 us)
Async XLA Ops:
  6.5 150.4 %all-gather.5.cloned.1.call-start = ((), (), s32[]{:S(2)}) async-start(), calls=%async_computation.3 | async-start | bytes 6684672 | tf_op jit(solution)/shard_map/all_gather | solution.py:107
  163.3 7.6 %copy-start.1 = (s32[1024,3]{0,1:T(4,128)S(1)}, s32[1024,3]{0,1:T(4,128)}, u32[]{:S(2)}) copy-start(s32[1024,3]{0,1:T(4,128)} %param.20) | copy-start | bytes 36868
  163.3 8.1 %copy-start.2 = (s32[1024,3]{0,1:T(4,128)S(1)}, s32[1024,3]{0,1:T(4,128)}, u32[]{:S(2)}) copy-start(s32[1024,3]{0,1:T(4,128)} %param.21) | copy-start | bytes 36868
  163.3 46.8 %all-to-all-start = ((bf16[256,16,192]{0,2,1:T(8,128)(2,1)}), bf16[256,16,192]{0,2,1:T(8,128)(2,1)S(1)}, u32[]{:S(2)}, u32[]{:S(2)}) async-start(bf16[256,16,192]{0,2,1:T(8,128)(2,1)} %convert_element_type.55), calls=%async_computation | async-start | bytes 3145728 | tf_op jit(solution)/shard_map/all_to_all | solution.py:110
  170.9 142.2 %all-gather.9.cloned.1.call-start = ((), (), s32[]{:S(2)}) async-start(), calls=%async_computation.5 | async-start | bytes 1081344 | tf_op jit(solution)/shard_map/all_gather | solution.py:31
  222.4 11.5 %copy-start.3 = (s32[1024]{0:T(1024)S(1)}, s32[1024]{0:T(1024)}, u32[]{:S(2)}) copy-start(s32[1024]{0:T(1024)} %param.19) | copy-start | bytes 12292
  222.4 110.7 %all-to-all-start.1 = ((bf16[32,4,128,128]{3,2,1,0:T(8,128)(2,1)}), bf16[32,4,128,128]{3,2,1,0:T(8,128)(2,1)}, u32[]{:S(2)}, u32[]{:S(2)}) async-start(bf16[32,4,128,128]{3,2,1,0:T(8,128)(2,1)} %bitcast.135), calls=%async_computation.1 | async-start | bytes 8388608 | tf_op jit(solution)/shard_map/all_to_all | solution.py:141
  233.1 179.9 %all-gather.7.cloned.1.call-start = ((), (), s32[]{:S(2)}) async-start(), calls=%async_computation.4 | async-start | bytes 2228224 | tf_op jit(solution)/shard_map/all_gather | solution.py:180
  240.3 8.2 %collective-permute-start = (bf16[128,128]{0,1:T(8,128)(2,1)S(1)}, bf16[128,128]{0,1:T(8,128)(2,1)S(1)}, u32[]{:S(2)}, u32[]{:S(2)}) collective-permute-start(bf16[128,128]{0,1:T(8,128)(2,1)S(1)} %get-tuple-element.200), channel_id=1, source_target_pairs={{0,16},{16,32},{32,48},{48,64},{64,80},{80,96},{96,112},{112,128},... | collective-permute-start | bytes 98312 | tf_op jit(solution)/shard_map/ppermute | solution.py:20
  242.3 7.9 %collective-permute-start.1 = (bf16[128,128]{0,1:T(8,128)(2,1)S(1)}, bf16[128,128]{0,1:T(8,128)(2,1)S(1)}, u32[]{:S(2)}, u32[]{:S(2)}) collective-permute-start(bf16[128,128]{0,1:T(8,128)(2,1)S(1)} %get-tuple-element.199), channel_id=1, source_target_pairs={{16,0},{32,16},{48,32},{64,48},{80,64},{96,80},{112,96},{128,112},... | collective-permute-start | bytes 98312 | tf_op jit(solution)/shard_map/ppermute | solution.py:22
  407.1 23.8 %copy-start = (f32[1024]{0:T(1024)S(1)}, f32[1024]{0:T(1024)}, u32[]{:S(2)}) copy-start(f32[1024]{0:T(1024)} %param.18) | copy-start | bytes 12292
  409.5 21.4 %all-to-all-start.2 = ((bf16[16,256,64]{1,2,0:T(8,128)(2,1)}), bf16[16,256,64]{1,2,0:T(8,128)(2,1)S(1)}, u32[]{:S(2)}, u32[]{:S(2)}) async-start(bf16[16,256,64]{1,2,0:T(8,128)(2,1)} %copy.46), calls=%async_computation.2 | async-start | bytes 1048576 | tf_op jit(solution)/shard_map/all_to_all | solution.py:177
Sparse Core Ops, SparseCore 0:
  9.4 147.4 all-gather.4
  216.9 96.1 all-gather.8
  315.1 77.5 all-gather.6
